TPU v7x, 256 devices: a whole 4x4x8 slice. The times are simulated.
256 devices in a mesh: row: 8 (over z), col: 32 (over y, x, core).
Axes of the slice: x: 4, y: 4, z: 8, core: 2. Of those that a mesh axis runs over, the one named last changes fastest.
Arguments:
- factor: bfloat16 [32, 8, 8, 32, 128, 128], P(None, 'row', None, 'col'), may hold values from -0.046875 to 0.046875
- pattern: int32 [32, 8, 8, 32], P(None, 'row', None, 'col'), may hold values 0 or 1
- loads: float32 [8, 32, 128, 256], P(None, 'col'), may hold values from -6 to 6
- block_inverse: float32 [8, 32, 128, 128], P(None, 'col'), may hold values from -1 to 2, as said below
Outputs:
- solution: float32 [8, 32, 128, 256], P(None, 'col')
Inputs may be any that keep to these rules, and one draw needn't show every extreme that they name: `block_inverse`: each block is lower triangular with diagonal entries between 0.5 and 1.5.
All inputs are finite; a program needn't handle non-finite values. No bound on the sum of `pattern` on one device may be relied on, other than what follows from the above.
Results may differ from a plain program's by a relative error of at most 0.0045.
Values may be sent and summed in bfloat16 or wider, within the bound.
No kernel may reach another device: no remote copies, remote signals or barrier semaphores. Data moves between devices by JAX's collectives and lax.ppermute only.
A program may use at most 128 MiB of HBM per device.

v0:
```python
import jax
import jax.numpy as jnp
from jax import lax
from jax.sharding import PartitionSpec as P

LEVELS = 8


def spread(value, axis, source):
    kept = jnp.where(lax.axis_index(axis) == source, value, 0).astype(value.dtype)
    return lax.psum(kept, axis)


def per_device(factor, pattern, loads, block_inverse):
    row_count = lax.axis_size("row")
    col_count = lax.axis_size("col")
    groups = col_count // row_count
    my_row = lax.axis_index("row")
    my_col = lax.axis_index("col")
    masked = factor[:, 0, :, 0] * pattern[:, 0, :, 0].astype(jnp.bfloat16)[:, :, None, None]
    per_row = factor.shape[0] // LEVELS
    per_col = factor.shape[2] // LEVELS
    rhs_local = loads[:, 0]
    inverse_local = block_inverse[:, 0]
    forward_vals = []
    forward_low = []
    for level_id in range(LEVELS):
        rhs_level = rhs_local[level_id * per_col : (level_id + 1) * per_col]
        inverse_level = inverse_local[level_id * per_col : (level_id + 1) * per_col]
        if level_id > 0:
            panel = masked[level_id * per_row : (level_id + 1) * per_row, : level_id * per_col]
            earlier = jnp.concatenate(forward_low, axis=0)
            partial_sum = jnp.einsum(
                "abpq,bqs->aps", panel, earlier, preferred_element_type=jnp.float32
            )
            row_total = lax.psum(partial_sum, "col")
            row_total = row_total.reshape((per_col, groups) + row_total.shape[1:])
            own_total = lax.dynamic_index_in_dim(
                row_total, my_col // row_count, axis=1, keepdims=False
            )
            solved = jnp.einsum(
                "mpq,mqs->mps",
                inverse_level,
                rhs_level - own_total,
                precision=lax.Precision.HIGHEST,
            )
            solved = spread(solved, "row", my_col % row_count)
        else:
            solved = jnp.einsum(
                "mpq,mqs->mps", inverse_level, rhs_level, precision=lax.Precision.HIGHEST
            )
        forward_vals.append(solved)
        forward_low.append(solved.astype(jnp.bfloat16))
    solution_parts = [None] * LEVELS
    later = []
    for level_id in reversed(range(LEVELS)):
        inverse_level = inverse_local[level_id * per_col : (level_id + 1) * per_col]
        resid = forward_vals[level_id]
        if level_id < LEVELS - 1:
            panel = masked[
                (level_id + 1) * per_row :, level_id * per_col : (level_id + 1) * per_col
            ]
            after = jnp.concatenate(later, axis=0)
            partial_sum = jnp.einsum(
                "abpq,aps->bqs", panel, after, preferred_element_type=jnp.float32
            )
            resid = resid - lax.psum(partial_sum, "row")
        solved = jnp.einsum("mqp,mqs->mps", inverse_level, resid, precision=lax.Precision.HIGHEST)
        solution_parts[level_id] = solved
        if level_id > 0:
            low_solved = solved.astype(jnp.bfloat16)
            pieces = lax.all_gather(low_solved[None], "col", axis=0, tiled=True)
            pieces = pieces.reshape((groups, row_count) + low_solved.shape)
            picked = lax.dynamic_index_in_dim(pieces, my_row, axis=1, keepdims=False)
            arranged = jnp.swapaxes(picked, 0, 1).reshape((per_row,) + low_solved.shape[1:])
            later = [arranged] + later
    solution = jnp.concatenate(solution_parts, axis=0)
    return solution[:, None]


def solution(mesh):
    in_specs = (
        P(None, "row", None, "col", None, None),
        P(None, "row", None, "col"),
        P(None, "col", None, None),
        P(None, "col", None, None),
    )
    out_specs = P(None, "col", None, None)
    return jax.shard_map(
        per_device, mesh=mesh, in_specs=in_specs, out_specs=out_specs, check_vma=False
    )
```

profile of v0, /device:TPU:2, one launch (start us, length us, event | category | flops | bytes accessed | tf_op | source)
XLA Modules:
  0.0 2246.1 jit_solution(3896068341786399089)
XLA Ops:
  8.5 7.4 bitcast_multiply_fusion
  17.9 116.1 %all-reduce.22.cloned.1.call-done = f32[4,128,256]{2,1,0:T(8,128)} async-done(((f32[4,128,256]{2,1,0:T(8,128)}), f32[4,128,256]{2,1,0:T(8,128)}) %all-reduce.22.cloned.1.call-update) | async-done | bytes 524304 | tf_op jit(solution)/shard_map/psum | solution.py:36
  135.9 72.4 %all-reduce.24.cloned.1.call-done = f32[1,128,256]{2,1,0:T(8,128)} async-done(((f32[1,128,256]{2,1,0:T(8,128)}), f32[1,128,256]{2,1,0:T(8,128)}) %all-reduce.24.cloned.1.call-update) | async-done | bytes 131088 | tf_op jit(solution)/shard_map/psum | solution.py:11
  209.3 2.0 convolution_bitcast_fusion.5
  211.3 111.8 %all-reduce.26.cloned.1.call-done = f32[4,128,256]{2,1,0:T(8,128)} async-done(((f32[4,128,256]{2,1,0:T(8,128)}), f32[4,128,256]{2,1,0:T(8,128)}) %all-reduce.26.cloned.1.call-update) | async-done | bytes 524304 | tf_op jit(solution)/shard_map/psum | solution.py:36
  325.1 72.3 %all-reduce.28.cloned.1.call-done = f32[1,128,256]{2,1,0:T(8,128)} async-done(((f32[1,128,256]{2,1,0:T(8,128)}), f32[1,128,256]{2,1,0:T(8,128)}) %all-reduce.28.cloned.1.call-update) | async-done | bytes 131088 | tf_op jit(solution)/shard_map/psum | solution.py:11
  398.3 2.1 convolution_bitcast_fusion.4
  400.5 111.6 %all-reduce.30.cloned.1.call-done = f32[4,128,256]{2,1,0:T(8,128)} async-done(((f32[4,128,256]{2,1,0:T(8,128)}), f32[4,128,256]{2,1,0:T(8,128)}) %all-reduce.30.cloned.1.call-update) | async-done | bytes 524304 | tf_op jit(solution)/shard_map/psum | solution.py:36
  514.0 72.3 %all-reduce.32.cloned.1.call-done = f32[1,128,256]{2,1,0:T(8,128)} async-done(((f32[1,128,256]{2,1,0:T(8,128)}), f32[1,128,256]{2,1,0:T(8,128)}) %all-reduce.32.cloned.1.call-update) | async-done | bytes 131088 | tf_op jit(solution)/shard_map/psum | solution.py:11
  587.3 2.1 convolution_bitcast_fusion.3
  589.5 111.6 %all-reduce.34.cloned.1.call-done = f32[4,128,256]{2,1,0:T(8,128)} async-done(((f32[4,128,256]{2,1,0:T(8,128)}), f32[4,128,256]{2,1,0:T(8,128)}) %all-reduce.34.cloned.1.call-update) | async-done | bytes 524304 | tf_op jit(solution)/shard_map/psum | solution.py:36
  703.1 72.4 %all-reduce.36.cloned.1.call-done = f32[1,128,256]{2,1,0:T(8,128)} async-done(((f32[1,128,256]{2,1,0:T(8,128)}), f32[1,128,256]{2,1,0:T(8,128)}) %all-reduce.36.cloned.1.call-update) | async-done | bytes 131088 | tf_op jit(solution)/shard_map/psum | solution.py:11
  776.4 2.3 convolution_bitcast_fusion.2
  778.8 111.6 %all-reduce.38.cloned.1.call-done = f32[4,128,256]{2,1,0:T(8,128)} async-done(((f32[4,128,256]{2,1,0:T(8,128)}), f32[4,128,256]{2,1,0:T(8,128)}) %all-reduce.38.cloned.1.call-update) | async-done | bytes 524304 | tf_op jit(solution)/shard_map/psum | solution.py:36
  892.3 72.3 %all-reduce.40.cloned.1.call-done = f32[1,128,256]{2,1,0:T(8,128)} async-done(((f32[1,128,256]{2,1,0:T(8,128)}), f32[1,128,256]{2,1,0:T(8,128)}) %all-reduce.40.cloned.1.call-update) | async-done | bytes 131088 | tf_op jit(solution)/shard_map/psum | solution.py:11
  965.6 2.3 convolution_bitcast_fusion.1
  967.9 111.7 %all-reduce.42.cloned.1.call-done = f32[4,128,256]{2,1,0:T(8,128)} async-done(((f32[4,128,256]{2,1,0:T(8,128)}), f32[4,128,256]{2,1,0:T(8,128)}) %all-reduce.42.cloned.1.call-update) | async-done | bytes 524304 | tf_op jit(solution)/shard_map/psum | solution.py:36
  1081.5 72.3 %all-reduce.44.cloned.1.call-done = f32[1,128,256]{2,1,0:T(8,128)} async-done(((f32[1,128,256]{2,1,0:T(8,128)}), f32[1,128,256]{2,1,0:T(8,128)}) %all-reduce.44.cloned.1.call-update) | async-done | bytes 131088 | tf_op jit(solution)/shard_map/psum | solution.py:11
  1154.8 2.4 convolution_bitcast_fusion
  1157.2 111.7 %all-reduce.46.cloned.1.call-done = f32[4,128,256]{2,1,0:T(8,128)} async-done(((f32[4,128,256]{2,1,0:T(8,128)}), f32[4,128,256]{2,1,0:T(8,128)}) %all-reduce.46.cloned.1.call-update) | async-done | bytes 524304 | tf_op jit(solution)/shard_map/psum | solution.py:36
  1270.8 72.3 %all-reduce.48.cloned.1.call-done = f32[128,256]{1,0:T(8,128)} async-done(((f32[128,256]{1,0:T(8,128)}), f32[128,256]{1,0:T(8,128)}) %all-reduce.48.cloned.1.call-update) | async-done | bytes 131088 | tf_op jit(solution)/shard_map/psum | solution.py:11
  1345.2 48.3 %all-gather.15.cloned.1.call-done = bf16[4096,256]{0,1:T(8,128)(2,1)} async-done(((bf16[128,256]{0,1:T(8,128)(2,1)}), bf16[4096,256]{0,1:T(8,128)(2,1)}) %all-gather.15.cloned.1.call-update) | async-done | bytes 2097168 | tf_op jit(solution)/shard_map/all_gather | solution.py:72
  1393.4 2.1 copy.59
  1398.4 71.8 %all-reduce.50.cloned.1.call-done = f32[1,128,256]{2,1,0:T(8,128)} async-done(((f32[1,128,256]{2,1,0:T(8,128)}), f32[1,128,256]{2,1,0:T(8,128)}) %all-reduce.50.cloned.1.call-update) | async-done | bytes 131088 | tf_op jit(solution)/shard_map/psum | solution.py:67
  1472.2 48.6 %all-gather.17.cloned.1.call-done = bf16[4096,256]{0,1:T(8,128)(2,1)} async-done(((bf16[128,256]{0,1:T(8,128)(2,1)}), bf16[4096,256]{0,1:T(8,128)(2,1)}) %all-gather.17.cloned.1.call-update) | async-done | bytes 2097168 | tf_op jit(solution)/shard_map/all_gather | solution.py:72
  1520.8 2.1 copy.60
  1525.9 71.8 %all-reduce.52.cloned.1.call-done = f32[1,128,256]{2,1,0:T(8,128)} async-done(((f32[1,128,256]{2,1,0:T(8,128)}), f32[1,128,256]{2,1,0:T(8,128)}) %all-reduce.52.cloned.1.call-update) | async-done | bytes 131088 | tf_op jit(solution)/shard_map/psum | solution.py:67
  1599.6 48.4 %all-gather.19.cloned.1.call-done = bf16[4096,256]{0,1:T(8,128)(2,1)} async-done(((bf16[128,256]{0,1:T(8,128)(2,1)}), bf16[4096,256]{0,1:T(8,128)(2,1)}) %all-gather.19.cloned.1.call-update) | async-done | bytes 2097168 | tf_op jit(solution)/shard_map/all_gather | solution.py:72
  1648.1 2.1 copy.61
  1651.2 2.0 convolution_bitcast_fusion.11
  1653.2 71.8 %all-reduce.54.cloned.1.call-done = f32[1,128,256]{2,1,0:T(8,128)} async-done(((f32[1,128,256]{2,1,0:T(8,128)}), f32[1,128,256]{2,1,0:T(8,128)}) %all-reduce.54.cloned.1.call-update) | async-done | bytes 131088 | tf_op jit(solution)/shard_map/psum | solution.py:67
  1727.2 48.6 %all-gather.21.cloned.1.call-done = bf16[4096,256]{0,1:T(8,128)(2,1)} async-done(((bf16[128,256]{0,1:T(8,128)(2,1)}), bf16[4096,256]{0,1:T(8,128)(2,1)}) %all-gather.21.cloned.1.call-update) | async-done | bytes 2097168 | tf_op jit(solution)/shard_map/all_gather | solution.py:72
  1775.8 2.1 copy.62
  1778.9 2.1 convolution_bitcast_fusion.13
  1781.1 71.8 %all-reduce.56.cloned.1.call-done = f32[1,128,256]{2,1,0:T(8,128)} async-done(((f32[1,128,256]{2,1,0:T(8,128)}), f32[1,128,256]{2,1,0:T(8,128)}) %all-reduce.56.cloned.1.call-update) | async-done | bytes 131088 | tf_op jit(solution)/shard_map/psum | solution.py:67
  1854.9 48.4 %all-gather.23.cloned.1.call-done = bf16[4096,256]{0,1:T(8,128)(2,1)} async-done(((bf16[128,256]{0,1:T(8,128)(2,1)}), bf16[4096,256]{0,1:T(8,128)(2,1)}) %all-gather.23.cloned.1.call-update) | async-done | bytes 2097168 | tf_op jit(solution)/shard_map/all_gather | solution.py:72
  1903.3 2.1 copy.63
  1906.5 2.1 convolution_bitcast_fusion.12
  1908.8 71.8 %all-reduce.58.cloned.1.call-done = f32[1,128,256]{2,1,0:T(8,128)} async-done(((f32[1,128,256]{2,1,0:T(8,128)}), f32[1,128,256]{2,1,0:T(8,128)}) %all-reduce.58.cloned.1.call-update) | async-done | bytes 131088 | tf_op jit(solution)/shard_map/psum | solution.py:67
  1980.5 2.0 bitcast_convert_fusion.1
  1982.6 48.7 %all-gather.25.cloned.1.call-done = bf16[4096,256]{0,1:T(8,128)(2,1)} async-done(((bf16[128,256]{0,1:T(8,128)(2,1)}), bf16[4096,256]{0,1:T(8,128)(2,1)}) %all-gather.25.cloned.1.call-update) | async-done | bytes 2097168 | tf_op jit(solution)/shard_map/all_gather | solution.py:72
  2031.3 2.1 copy.64
  2034.5 2.2 convolution_bitcast_fusion.7
  2036.8 71.8 %all-reduce.60.cloned.1.call-done = f32[1,128,256]{2,1,0:T(8,128)} async-done(((f32[1,128,256]{2,1,0:T(8,128)}), f32[1,128,256]{2,1,0:T(8,128)}) %all-reduce.60.cloned.1.call-update) | async-done | bytes 131088 | tf_op jit(solution)/shard_map/psum | solution.py:67
  2110.7 48.2 %all-gather.27.cloned.1.call-done = bf16[4096,256]{0,1:T(8,128)(2,1)} async-done(((bf16[128,256]{0,1:T(8,128)(2,1)}), bf16[4096,256]{0,1:T(8,128)(2,1)}) %all-gather.27.cloned.1.call-update) | async-done | bytes 2097168 | tf_op jit(solution)/shard_map/all_gather | solution.py:72
  2158.9 2.1 copy.65
  2162.2 2.4 convolution_bitcast_fusion.6
  2164.6 71.8 %all-reduce.62.cloned.1.call-done = f32[1,128,256]{2,1,0:T(8,128)} async-done(((f32[1,128,256]{2,1,0:T(8,128)}), f32[1,128,256]{2,1,0:T(8,128)}) %all-reduce.62.cloned.1.call-update) | async-done | bytes 131088 | tf_op jit(solution)/shard_map/psum | solution.py:67
  (149 shorter events, 49.5 us)
Async XLA Ops:
  6.5 127.4 %all-reduce.22.cloned.1.call-start = ((), (), s32[]{:S(2)}) async-start(), calls=%async_computation | async-start | bytes 1048576 | tf_op jit(solution)/shard_map/psum | solution.py:36
  8.4 125.5 %copy-start = (f32[8,1,128,128]{3,2,1,0:T(8,128)S(1)}, f32[8,1,128,128]{3,2,1,0:T(8,128)}, u32[]{:S(2)}) copy-start(f32[8,1,128,128]{3,2,1,0:T(8,128)} %param.7) | copy-start | bytes 1572868
  8.5 125.5 %copy-start.1 = (f32[8,1,128,256]{3,2,1,0:T(8,128)S(1)}, f32[8,1,128,256]{3,2,1,0:T(8,128)}, u32[]{:S(2)}) copy-start(f32[8,1,128,256]{3,2,1,0:T(8,128)} %param.6) | copy-start | bytes 3145732
  17.8 190.6 %all-reduce.24.cloned.1.call-start = ((), (), s32[]{:S(2)}) async-start(), calls=%async_computation.1 | async-start | bytes 262144 | tf_op jit(solution)/shard_map/psum | solution.py:11
  135.8 187.3 %all-reduce.26.cloned.1.call-start = ((), (), s32[]{:S(2)}) async-start(), calls=%async_computation.2 | async-start | bytes 1048576 | tf_op jit(solution)/shard_map/psum | solution.py:36
  211.3 186.1 %all-reduce.28.cloned.1.call-start = ((), (), s32[]{:S(2)}) async-start(), calls=%async_computation.3 | async-start | bytes 262144 | tf_op jit(solution)/shard_map/psum | solution.py:11
  325.0 187.1 %all-reduce.30.cloned.1.call-start = ((), (), s32[]{:S(2)}) async-start(), calls=%async_computation.4 | async-start | bytes 1048576 | tf_op jit(solution)/shard_map/psum | solution.py:36
  400.4 185.9 %all-reduce.32.cloned.1.call-start = ((), (), s32[]{:S(2)}) async-start(), calls=%async_computation.5 | async-start | bytes 262144 | tf_op jit(solution)/shard_map/psum | solution.py:11
  514.0 187.1 %all-reduce.34.cloned.1.call-start = ((), (), s32[]{:S(2)}) async-start(), calls=%async_computation.6 | async-start | bytes 1048576 | tf_op jit(solution)/shard_map/psum | solution.py:36
  589.4 186.1 %all-reduce.36.cloned.1.call-start = ((), (), s32[]{:S(2)}) async-start(), calls=%async_computation.7 | async-start | bytes 262144 | tf_op jit(solution)/shard_map/psum | solution.py:11
  703.0 187.4 %all-reduce.38.cloned.1.call-start = ((), (), s32[]{:S(2)}) async-start(), calls=%async_computation.8 | async-start | bytes 1048576 | tf_op jit(solution)/shard_map/psum | solution.py:36
  778.7 185.9 %all-reduce.40.cloned.1.call-start = ((), (), s32[]{:S(2)}) async-start(), calls=%async_computation.9 | async-start | bytes 262144 | tf_op jit(solution)/shard_map/psum | solution.py:11
  892.3 187.3 %all-reduce.42.cloned.1.call-start = ((), (), s32[]{:S(2)}) async-start(), calls=%async_computation.10 | async-start | bytes 1048576 | tf_op jit(solution)/shard_map/psum | solution.py:36
  967.9 186.0 %all-reduce.44.cloned.1.call-start = ((), (), s32[]{:S(2)}) async-start(), calls=%async_computation.11 | async-start | bytes 262144 | tf_op jit(solution)/shard_map/psum | solution.py:11
  1081.5 187.4 %all-reduce.46.cloned.1.call-start = ((), (), s32[]{:S(2)}) async-start(), calls=%async_computation.12 | async-start | bytes 1048576 | tf_op jit(solution)/shard_map/psum | solution.py:36
  1157.2 186.0 %all-reduce.48.cloned.1.call-start = ((), (), s32[]{:S(2)}) async-start(), calls=%async_computation.13 | async-start | bytes 262144 | tf_op jit(solution)/shard_map/psum | solution.py:11
  1270.8 122.7 %all-gather.15.cloned.1.call-start = ((), (), s32[]{:S(2)}) async-start(), calls=%async_computation.21 | async-start | bytes 2162688 | tf_op jit(solution)/shard_map/all_gather | solution.py:72
  1345.1 125.1 %all-reduce.50.cloned.1.call-start = ((), (), s32[]{:S(2)}) async-start(), calls=%async_computation.14 | async-start | bytes 262144 | tf_op jit(solution)/shard_map/psum | solution.py:67
  1395.5 74.7 %copy-start.9 = (f32[1,128,256]{2,1,0:T(8,128)S(1)}, f32[1,128,256]{2,1,0:T(8,128)}, u32[]{:S(2)}) copy-start(f32[1,128,256]{2,1,0:T(8,128)} %all-reduce.44.cloned.1.call-done) | copy-start | bytes 393220
  1398.4 122.4 %all-gather.17.cloned.1.call-start = ((), (), s32[]{:S(2)}) async-start(), calls=%async_computation.22 | async-start | bytes 2162688 | tf_op jit(solution)/shard_map/all_gather | solution.py:72
  1472.1 125.5 %all-reduce.52.cloned.1.call-start = ((), (), s32[]{:S(2)}) async-start(), calls=%async_computation.15 | async-start | bytes 262144 | tf_op jit(solution)/shard_map/psum | solution.py:67
  1522.9 74.8 %copy-start.6 = (f32[1,128,256]{2,1,0:T(8,128)S(1)}, f32[1,128,256]{2,1,0:T(8,128)}, u32[]{:S(2)}) copy-start(f32[1,128,256]{2,1,0:T(8,128)} %all-reduce.40.cloned.1.call-done) | copy-start | bytes 393220
  1525.8 122.3 %all-gather.19.cloned.1.call-start = ((), (), s32[]{:S(2)}) async-start(), calls=%async_computation.23 | async-start | bytes 2162688 | tf_op jit(solution)/shard_map/all_gather | solution.py:72
  1599.6 125.4 %all-reduce.54.cloned.1.call-start = ((), (), s32[]{:S(2)}) async-start(), calls=%async_computation.16 | async-start | bytes 262144 | tf_op jit(solution)/shard_map/psum | solution.py:67
  1650.7 74.3 %copy-start.5 = (f32[1,128,256]{2,1,0:T(8,128)S(1)}, f32[1,128,256]{2,1,0:T(8,128)}, u32[]{:S(2)}) copy-start(f32[1,128,256]{2,1,0:T(8,128)} %all-reduce.36.cloned.1.call-done) | copy-start | bytes 393220
  1653.2 122.6 %all-gather.21.cloned.1.call-start = ((), (), s32[]{:S(2)}) async-start(), calls=%async_computation.24 | async-start | bytes 2162688 | tf_op jit(solution)/shard_map/all_gather | solution.py:72
  1727.0 125.9 %all-reduce.56.cloned.1.call-start = ((), (), s32[]{:S(2)}) async-start(), calls=%async_computation.17 | async-start | bytes 262144 | tf_op jit(solution)/shard_map/psum | solution.py:67
  1778.9 74.0 %copy-start.4 = (f32[1,128,256]{2,1,0:T(8,128)S(1)}, f32[1,128,256]{2,1,0:T(8,128)}, u32[]{:S(2)}) copy-start(f32[1,128,256]{2,1,0:T(8,128)} %all-reduce.32.cloned.1.call-done) | copy-start | bytes 393220
  1781.0 122.3 %all-gather.23.cloned.1.call-start = ((), (), s32[]{:S(2)}) async-start(), calls=%async_computation.25 | async-start | bytes 2162688 | tf_op jit(solution)/shard_map/all_gather | solution.py:72
  1854.8 125.7 %all-reduce.58.cloned.1.call-start = ((), (), s32[]{:S(2)}) async-start(), calls=%async_computation.18 | async-start | bytes 262144 | tf_op jit(solution)/shard_map/psum | solution.py:67
  1906.5 74.1 %copy-start.3 = (f32[1,128,256]{2,1,0:T(8,128)S(1)}, f32[1,128,256]{2,1,0:T(8,128)}, u32[]{:S(2)}) copy-start(f32[1,128,256]{2,1,0:T(8,128)} %all-reduce.28.cloned.1.call-done) | copy-start | bytes 393220
  1908.7 122.6 %all-gather.25.cloned.1.call-start = ((), (), s32[]{:S(2)}) async-start(), calls=%async_computation.26 | async-start | bytes 2162688 | tf_op jit(solution)/shard_map/all_gather | solution.py:72
  1982.5 126.1 %all-reduce.60.cloned.1.call-start = ((), (), s32[]{:S(2)}) async-start(), calls=%async_computation.19 | async-start | bytes 262144 | tf_op jit(solution)/shard_map/psum | solution.py:67
  2034.5 74.1 %copy-start.2 = (f32[1,128,256]{2,1,0:T(8,128)S(1)}, f32[1,128,256]{2,1,0:T(8,128)}, u32[]{:S(2)}) copy-start(f32[1,128,256]{2,1,0:T(8,128)} %all-reduce.24.cloned.1.call-done) | copy-start | bytes 393220
  2036.8 122.1 %all-gather.27.cloned.1.call-start = ((), (), s32[]{:S(2)}) async-start(), calls=%async_computation.27 | async-start | bytes 2162688 | tf_op jit(solution)/shard_map/all_gather | solution.py:72
  2110.6 125.8 %all-reduce.62.cloned.1.call-start = ((), (), s32[]{:S(2)}) async-start(), calls=%async_computation.20 | async-start | bytes 262144 | tf_op jit(solution)/shard_map/psum | solution.py:67
  2162.2 75.5 %copy-start.10 = (f32[256,128]{1,0:T(8,128)S(1)}, f32[256,128]{1,0:T(8,128)}, u32[]{:S(2)}) copy-start(f32[256,128]{1,0:T(8,128)} %get-tuple-element.39) | copy-start | bytes 393220
  2162.2 75.6 %copy-start.8 = (f32[256,128]{1,0:T(8,128)S(1)}, f32[256,128]{1,0:T(8,128)}, u32[]{:S(2)}) copy-start(f32[256,128]{1,0:T(8,128)} %get-tuple-element.37) | copy-start | bytes 393220
  2162.2 75.6 %copy-start.7 = (f32[256,128]{1,0:T(8,128)S(1)}, f32[256,128]{1,0:T(8,128)}, u32[]{:S(2)}) copy-start(f32[256,128]{1,0:T(8,128)} %get-tuple-element.35) | copy-start | bytes 393220
Sparse Core Ops, SparseCore 0:
  17.9 116.0 all-reduce.21
  136.4 71.9 all-reduce.23
  211.6 111.5 all-reduce.25
  325.4 71.9 all-reduce.27
  400.5 111.5 all-reduce.29
  514.4 71.9 all-reduce.31
  589.5 111.5 all-reduce.33
  703.5 71.9 all-reduce.35
  778.8 111.5 all-reduce.37
  892.7 71.9 all-reduce.39
  968.0 111.5 all-reduce.41
  1081.9 71.9 all-reduce.43
  1157.3 111.5 all-reduce.45
  1271.2 71.9 all-reduce.47
  1345.5 47.9 all-gather.14
  1398.5 71.6 all-reduce.49
  1472.8 47.9 all-gather.16
  1525.9 71.6 all-reduce.51
  1600.1 47.9 all-gather.18
  1653.3 71.6 all-reduce.53
  1727.8 47.9 all-gather.20
  1781.1 71.6 all-reduce.55
  1855.3 47.9 all-gather.22
  1908.8 71.6 all-reduce.57
  1983.3 47.9 all-gather.24
  2036.9 71.6 all-reduce.59
  2110.9 47.9 all-gather.26
  2164.7 71.6 all-reduce.61
where the time goes:
time: 2250 us
  waiting for transfers between devices  2130 us (95%)
  matrix products  58.4 us (3%)
  local copies, waits for them, and re-layouts  23.5 us (1%)
    psum x7, waiting for transfers between devices, per_device(): row_total = lax.psum(partial_sum, 'col')  786 us
    psum x7, waiting for transfers between devices, spread(): return lax.psum(kept, axis)  507 us
    psum x7, waiting for transfers between devices, per_device(): resid = resid - lax.psum(partial_sum, 'row')  502 us
    all_gather x7, waiting for transfers between devices, per_device(): pieces = lax.all_gather(low_solved[None], 'col', axis=0, tiled=True)  339 us
  transfers between devices with their start and end apart: 28, of which 28 were waited for; matrix products, arithmetic and copies ran while one was open for 0% of the time, Pallas kernels for 0%

commit v1 on v0

--- a/solution.py
+++ b/solution.py
@@ -8,7 +8,7 @@
 
 def spread(value, axis, source):
     kept = jnp.where(lax.axis_index(axis) == source, value, 0).astype(value.dtype)
-    return lax.psum(kept, axis)
+    return jnp.sum(lax.all_gather(kept, axis), axis=0)
 
 
 def per_device(factor, pattern, loads, block_inverse):

time: 2250 us -> 2030 us (0.902)
  waiting for transfers between devices: 2130 us -> 1910 us
    psum x7 -> x0, waiting for transfers between devices: 507 us -> none  [spread(): return lax.psum(kept, axis)]
    all_gather x0 -> x7, waiting for transfers between devices: none -> 276 us  [spread(): return jnp.sum(lax.all_gather(kept, axis), axis=0)]
where the time goes in v1:
time: 2030 us
  waiting for transfers between devices  1910 us (94%)
  matrix products  58.3 us (3%)
  local copies, waits for them, and re-layouts  36.4 us (2%)
    psum x7, waiting for transfers between devices, per_device(): row_total = lax.psum(partial_sum, 'col')  790 us
    psum x7, waiting for transfers between devices, per_device(): resid = resid - lax.psum(partial_sum, 'row')  502 us
    all_gather x7, waiting for transfers between devices, per_device(): pieces = lax.all_gather(low_solved[None], 'col', axis=0, tiled=True)  340 us
    all_gather x7, waiting for transfers between devices, spread(): return jnp.sum(lax.all_gather(kept, axis), axis=0)  276 us
  transfers between devices with their start and end apart: 28, of which 28 were waited for; matrix products, arithmetic and copies ran while one was open for 0% of the time, Pallas kernels for 0%

profile of v1, /device:TPU:2, one launch (start us, length us, event | category | flops | bytes accessed | tf_op | source)
XLA Modules:
  0.0 2029.9 jit_solution(16727765825174284800)
XLA Ops:
  8.5 7.4 bitcast_multiply_fusion
  17.9 116.1 %all-reduce.15.cloned.1.call-done = f32[4,128,256]{2,1,0:T(8,128)} async-done(((f32[4,128,256]{2,1,0:T(8,128)}), f32[4,128,256]{2,1,0:T(8,128)}) %all-reduce.15.cloned.1.call-update) | async-done | bytes 524304 | tf_op jit(solution)/shard_map/psum | solution.py:36
  136.0 39.8 %all-gather.29.cloned.1.call-done = f32[1024,256]{0,1:T(8,128)} async-done(((f32[128,256]{0,1:T(8,128)}), f32[1024,256]{0,1:T(8,128)}) %all-gather.29.cloned.1.call-update) | async-done | bytes 1048592 | tf_op jit(solution)/shard_map/all_gather | solution.py:11
  177.6 2.0 convolution_bitcast_fusion.5
  179.6 112.4 %all-reduce.17.cloned.1.call-done = f32[4,128,256]{2,1,0:T(8,128)} async-done(((f32[4,128,256]{2,1,0:T(8,128)}), f32[4,128,256]{2,1,0:T(8,128)}) %all-reduce.17.cloned.1.call-update) | async-done | bytes 524304 | tf_op jit(solution)/shard_map/psum | solution.py:36
  294.0 39.8 %all-gather.31.cloned.1.call-done = f32[1024,256]{0,1:T(8,128)} async-done(((f32[128,256]{0,1:T(8,128)}), f32[1024,256]{0,1:T(8,128)}) %all-gather.31.cloned.1.call-update) | async-done | bytes 1048592 | tf_op jit(solution)/shard_map/all_gather | solution.py:11
  335.6 2.1 convolution_bitcast_fusion.4
  337.7 112.4 %all-reduce.19.cloned.1.call-done = f32[4,128,256]{2,1,0:T(8,128)} async-done(((f32[4,128,256]{2,1,0:T(8,128)}), f32[4,128,256]{2,1,0:T(8,128)}) %all-reduce.19.cloned.1.call-update) | async-done | bytes 524304 | tf_op jit(solution)/shard_map/psum | solution.py:36
  452.1 39.8 %all-gather.33.cloned.1.call-done = f32[1024,256]{0,1:T(8,128)} async-done(((f32[128,256]{0,1:T(8,128)}), f32[1024,256]{0,1:T(8,128)}) %all-gather.33.cloned.1.call-update) | async-done | bytes 1048592 | tf_op jit(solution)/shard_map/all_gather | solution.py:11
  493.7 2.1 convolution_bitcast_fusion.3
  495.9 112.4 %all-reduce.21.cloned.1.call-done = f32[4,128,256]{2,1,0:T(8,128)} async-done(((f32[4,128,256]{2,1,0:T(8,128)}), f32[4,128,256]{2,1,0:T(8,128)}) %all-reduce.21.cloned.1.call-update) | async-done | bytes 524304 | tf_op jit(solution)/shard_map/psum | solution.py:36
  612.8 37.2 %all-gather.35.cloned.1.call-done = f32[1024,256]{0,1:T(8,128)} async-done(((f32[128,256]{0,1:T(8,128)}), f32[1024,256]{0,1:T(8,128)}) %all-gather.35.cloned.1.call-update) | async-done | bytes 1048592 | tf_op jit(solution)/shard_map/all_gather | solution.py:11
  652.5 2.3 convolution_bitcast_fusion.2
  654.9 112.4 %all-reduce.23.cloned.1.call-done = f32[4,128,256]{2,1,0:T(8,128)} async-done(((f32[4,128,256]{2,1,0:T(8,128)}), f32[4,128,256]{2,1,0:T(8,128)}) %all-reduce.23.cloned.1.call-update) | async-done | bytes 524304 | tf_op jit(solution)/shard_map/psum | solution.py:36
  769.3 39.8 %all-gather.37.cloned.1.call-done = f32[1024,256]{0,1:T(8,128)} async-done(((f32[128,256]{0,1:T(8,128)}), f32[1024,256]{0,1:T(8,128)}) %all-gather.37.cloned.1.call-update) | async-done | bytes 1048592 | tf_op jit(solution)/shard_map/all_gather | solution.py:11
  810.9 2.3 convolution_bitcast_fusion.1
  813.3 112.4 %all-reduce.25.cloned.1.call-done = f32[4,128,256]{2,1,0:T(8,128)} async-done(((f32[4,128,256]{2,1,0:T(8,128)}), f32[4,128,256]{2,1,0:T(8,128)}) %all-reduce.25.cloned.1.call-update) | async-done | bytes 524304 | tf_op jit(solution)/shard_map/psum | solution.py:36
  927.6 39.8 %all-gather.39.cloned.1.call-done = f32[1024,256]{0,1:T(8,128)} async-done(((f32[128,256]{0,1:T(8,128)}), f32[1024,256]{0,1:T(8,128)}) %all-gather.39.cloned.1.call-update) | async-done | bytes 1048592 | tf_op jit(solution)/shard_map/all_gather | solution.py:11
  969.2 2.4 convolution_bitcast_fusion
  971.7 112.4 %all-reduce.27.cloned.1.call-done = f32[4,128,256]{2,1,0:T(8,128)} async-done(((f32[4,128,256]{2,1,0:T(8,128)}), f32[4,128,256]{2,1,0:T(8,128)}) %all-reduce.27.cloned.1.call-update) | async-done | bytes 524304 | tf_op jit(solution)/shard_map/psum | solution.py:36
  1086.1 39.8 %all-gather.41.cloned.1.call-done = f32[1024,256]{0,1:T(8,128)} async-done(((f32[128,256]{0,1:T(8,128)}), f32[1024,256]{0,1:T(8,128)}) %all-gather.41.cloned.1.call-update) | async-done | bytes 1048592 | tf_op jit(solution)/shard_map/all_gather | solution.py:11
  1128.5 48.7 %all-gather.43.cloned.1.call-done = bf16[4096,256]{0,1:T(8,128)(2,1)} async-done(((bf16[128,256]{0,1:T(8,128)(2,1)}), bf16[4096,256]{0,1:T(8,128)(2,1)}) %all-gather.43.cloned.1.call-update) | async-done | bytes 2097168 | tf_op jit(solution)/shard_map/all_gather | solution.py:72
  1177.3 2.1 copy.82
  1182.2 71.8 %all-reduce.29.cloned.1.call-done = f32[1,128,256]{2,1,0:T(8,128)} async-done(((f32[1,128,256]{2,1,0:T(8,128)}), f32[1,128,256]{2,1,0:T(8,128)}) %all-reduce.29.cloned.1.call-update) | async-done | bytes 131088 | tf_op jit(solution)/shard_map/psum | solution.py:67
  1256.2 48.1 %all-gather.45.cloned.1.call-done = bf16[4096,256]{0,1:T(8,128)(2,1)} async-done(((bf16[128,256]{0,1:T(8,128)(2,1)}), bf16[4096,256]{0,1:T(8,128)(2,1)}) %all-gather.45.cloned.1.call-update) | async-done | bytes 2097168 | tf_op jit(solution)/shard_map/all_gather | solution.py:72
  1304.3 2.1 copy.83
  1309.4 71.8 %all-reduce.31.cloned.1.call-done = f32[1,128,256]{2,1,0:T(8,128)} async-done(((f32[1,128,256]{2,1,0:T(8,128)}), f32[1,128,256]{2,1,0:T(8,128)}) %all-reduce.31.cloned.1.call-update) | async-done | bytes 131088 | tf_op jit(solution)/shard_map/psum | solution.py:67
  1383.1 48.7 %all-gather.47.cloned.1.call-done = bf16[4096,256]{0,1:T(8,128)(2,1)} async-done(((bf16[128,256]{0,1:T(8,128)(2,1)}), bf16[4096,256]{0,1:T(8,128)(2,1)}) %all-gather.47.cloned.1.call-update) | async-done | bytes 2097168 | tf_op jit(solution)/shard_map/all_gather | solution.py:72
  1431.9 2.1 copy.84
  1435.0 2.0 convolution_bitcast_fusion.11
  1437.0 71.8 %all-reduce.33.cloned.1.call-done = f32[1,128,256]{2,1,0:T(8,128)} async-done(((f32[1,128,256]{2,1,0:T(8,128)}), f32[1,128,256]{2,1,0:T(8,128)}) %all-reduce.33.cloned.1.call-update) | async-done | bytes 131088 | tf_op jit(solution)/shard_map/psum | solution.py:67
  1510.8 48.4 %all-gather.49.cloned.1.call-done = bf16[4096,256]{0,1:T(8,128)(2,1)} async-done(((bf16[128,256]{0,1:T(8,128)(2,1)}), bf16[4096,256]{0,1:T(8,128)(2,1)}) %all-gather.49.cloned.1.call-update) | async-done | bytes 2097168 | tf_op jit(solution)/shard_map/all_gather | solution.py:72
  1559.2 2.1 copy.85
  1562.4 2.1 convolution_bitcast_fusion.13
  1564.5 71.8 %all-reduce.35.cloned.1.call-done = f32[1,128,256]{2,1,0:T(8,128)} async-done(((f32[1,128,256]{2,1,0:T(8,128)}), f32[1,128,256]{2,1,0:T(8,128)}) %all-reduce.35.cloned.1.call-update) | async-done | bytes 131088 | tf_op jit(solution)/shard_map/psum | solution.py:67
  1638.3 48.7 %all-gather.51.cloned.1.call-done = bf16[4096,256]{0,1:T(8,128)(2,1)} async-done(((bf16[128,256]{0,1:T(8,128)(2,1)}), bf16[4096,256]{0,1:T(8,128)(2,1)}) %all-gather.51.cloned.1.call-update) | async-done | bytes 2097168 | tf_op jit(solution)/shard_map/all_gather | solution.py:72
  1687.0 2.1 copy.86
  1690.3 2.2 convolution_bitcast_fusion.12
  1692.5 71.8 %all-reduce.37.cloned.1.call-done = f32[1,128,256]{2,1,0:T(8,128)} async-done(((f32[1,128,256]{2,1,0:T(8,128)}), f32[1,128,256]{2,1,0:T(8,128)}) %all-reduce.37.cloned.1.call-update) | async-done | bytes 131088 | tf_op jit(solution)/shard_map/psum | solution.py:67
  1766.3 48.4 %all-gather.53.cloned.1.call-done = bf16[4096,256]{0,1:T(8,128)(2,1)} async-done(((bf16[128,256]{0,1:T(8,128)(2,1)}), bf16[4096,256]{0,1:T(8,128)(2,1)}) %all-gather.53.cloned.1.call-update) | async-done | bytes 2097168 | tf_op jit(solution)/shard_map/all_gather | solution.py:72
  1814.7 2.1 copy.87
  1818.0 2.2 convolution_bitcast_fusion.7
  1820.3 71.8 %all-reduce.39.cloned.1.call-done = f32[1,128,256]{2,1,0:T(8,128)} async-done(((f32[1,128,256]{2,1,0:T(8,128)}), f32[1,128,256]{2,1,0:T(8,128)}) %all-reduce.39.cloned.1.call-update) | async-done | bytes 131088 | tf_op jit(solution)/shard_map/psum | solution.py:67
  1892.1 2.0 bitcast_convert_fusion
  1894.1 48.6 %all-gather.55.cloned.1.call-done = bf16[4096,256]{0,1:T(8,128)(2,1)} async-done(((bf16[128,256]{0,1:T(8,128)(2,1)}), bf16[4096,256]{0,1:T(8,128)(2,1)}) %all-gather.55.cloned.1.call-update) | async-done | bytes 2097168 | tf_op jit(solution)/shard_map/all_gather | solution.py:72
  1942.7 2.1 copy.88
  1946.0 2.4 convolution_bitcast_fusion.6
  1948.4 71.8 %all-reduce.41.cloned.1.call-done = f32[1,128,256]{2,1,0:T(8,128)} async-done(((f32[1,128,256]{2,1,0:T(8,128)}), f32[1,128,256]{2,1,0:T(8,128)}) %all-reduce.41.cloned.1.call-update) | async-done | bytes 131088 | tf_op jit(solution)/shard_map/psum | solution.py:67
  (159 shorter events, 59.3 us)
Async XLA Ops:
  6.5 127.4 %all-reduce.15.cloned.1.call-start = ((), (), s32[]{:S(2)}) async-start(), calls=%async_computation | async-start | bytes 1048576 | tf_op jit(solution)/shard_map/psum | solution.py:36
  8.4 125.5 %copy-start = (f32[8,1,128,128]{3,2,1,0:T(8,128)S(1)}, f32[8,1,128,128]{3,2,1,0:T(8,128)}, u32[]{:S(2)}) copy-start(f32[8,1,128,128]{3,2,1,0:T(8,128)} %param.7) | copy-start | bytes 1572868
  8.5 125.5 %copy-start.1 = (f32[8,1,128,256]{3,2,1,0:T(8,128)S(1)}, f32[8,1,128,256]{3,2,1,0:T(8,128)}, u32[]{:S(2)}) copy-start(f32[8,1,128,256]{3,2,1,0:T(8,128)} %param.6) | copy-start | bytes 3145732
  17.8 158.0 %all-gather.29.cloned.1.call-start = ((), (), s32[]{:S(2)}) async-start(), calls=%async_computation.14 | async-start | bytes 1179648 | tf_op jit(solution)/shard_map/all_gather | solution.py:11
  135.9 156.0 %all-reduce.17.cloned.1.call-start = ((), (), s32[]{:S(2)}) async-start(), calls=%async_computation.1 | async-start | bytes 1048576 | tf_op jit(solution)/shard_map/psum | solution.py:36
  179.6 154.2 %all-gather.31.cloned.1.call-start = ((), (), s32[]{:S(2)}) async-start(), calls=%async_computation.15 | async-start | bytes 1179648 | tf_op jit(solution)/shard_map/all_gather | solution.py:11
  293.9 156.2 %all-reduce.19.cloned.1.call-start = ((), (), s32[]{:S(2)}) async-start(), calls=%async_computation.2 | async-start | bytes 1048576 | tf_op jit(solution)/shard_map/psum | solution.py:36
  337.7 154.2 %all-gather.33.cloned.1.call-start = ((), (), s32[]{:S(2)}) async-start(), calls=%async_computation.16 | async-start | bytes 1179648 | tf_op jit(solution)/shard_map/all_gather | solution.py:11
  452.1 156.2 %all-reduce.21.cloned.1.call-start = ((), (), s32[]{:S(2)}) async-start(), calls=%async_computation.3 | async-start | bytes 1048576 | tf_op jit(solution)/shard_map/psum | solution.py:36
  495.9 154.2 %all-gather.35.cloned.1.call-start = ((), (), s32[]{:S(2)}) async-start(), calls=%async_computation.17 | async-start | bytes 1179648 | tf_op jit(solution)/shard_map/all_gather | solution.py:11
  610.3 157.0 %all-reduce.23.cloned.1.call-start = ((), (), s32[]{:S(2)}) async-start(), calls=%async_computation.4 | async-start | bytes 1048576 | tf_op jit(solution)/shard_map/psum | solution.py:36
  654.9 154.2 %all-gather.37.cloned.1.call-start = ((), (), s32[]{:S(2)}) async-start(), calls=%async_computation.18 | async-start | bytes 1179648 | tf_op jit(solution)/shard_map/all_gather | solution.py:11
  769.2 156.4 %all-reduce.25.cloned.1.call-start = ((), (), s32[]{:S(2)}) async-start(), calls=%async_computation.5 | async-start | bytes 1048576 | tf_op jit(solution)/shard_map/psum | solution.py:36
  813.2 154.2 %all-gather.39.cloned.1.call-start = ((), (), s32[]{:S(2)}) async-start(), calls=%async_computation.19 | async-start | bytes 1179648 | tf_op jit(solution)/shard_map/all_gather | solution.py:11
  927.6 156.5 %all-reduce.27.cloned.1.call-start = ((), (), s32[]{:S(2)}) async-start(), calls=%async_computation.6 | async-start | bytes 1048576 | tf_op jit(solution)/shard_map/psum | solution.py:36
  971.7 154.2 %all-gather.41.cloned.1.call-start = ((), (), s32[]{:S(2)}) async-start(), calls=%async_computation.20 | async-start | bytes 1179648 | tf_op jit(solution)/shard_map/all_gather | solution.py:11
  1086.1 91.2 %all-gather.43.cloned.1.call-start = ((), (), s32[]{:S(2)}) async-start(), calls=%async_computation.21 | async-start | bytes 2162688 | tf_op jit(solution)/shard_map/all_gather | solution.py:72
  1128.5 125.5 %all-reduce.29.cloned.1.call-start = ((), (), s32[]{:S(2)}) async-start(), calls=%async_computation.7 | async-start | bytes 262144 | tf_op jit(solution)/shard_map/psum | solution.py:67
  1182.2 122.1 %all-gather.45.cloned.1.call-start = ((), (), s32[]{:S(2)}) async-start(), calls=%async_computation.22 | async-start | bytes 2162688 | tf_op jit(solution)/shard_map/all_gather | solution.py:72
  1256.0 125.2 %all-reduce.31.cloned.1.call-start = ((), (), s32[]{:S(2)}) async-start(), calls=%async_computation.8 | async-start | bytes 262144 | tf_op jit(solution)/shard_map/psum | solution.py:67
  1309.3 122.6 %all-gather.47.cloned.1.call-start = ((), (), s32[]{:S(2)}) async-start(), calls=%async_computation.23 | async-start | bytes 2162688 | tf_op jit(solution)/shard_map/all_gather | solution.py:72
  1383.1 125.7 %all-reduce.33.cloned.1.call-start = ((), (), s32[]{:S(2)}) async-start(), calls=%async_computation.9 | async-start | bytes 262144 | tf_op jit(solution)/shard_map/psum | solution.py:67
  1437.0 122.3 %all-gather.49.cloned.1.call-start = ((), (), s32[]{:S(2)}) async-start(), calls=%async_computation.24 | async-start | bytes 2162688 | tf_op jit(solution)/shard_map/all_gather | solution.py:72
  1510.8 125.5 %all-reduce.35.cloned.1.call-start = ((), (), s32[]{:S(2)}) async-start(), calls=%async_computation.10 | async-start | bytes 262144 | tf_op jit(solution)/shard_map/psum | solution.py:67
  1564.5 122.6 %all-gather.51.cloned.1.call-start = ((), (), s32[]{:S(2)}) async-start(), calls=%async_computation.25 | async-start | bytes 2162688 | tf_op jit(solution)/shard_map/all_gather | solution.py:72
  1638.3 126.0 %all-reduce.37.cloned.1.call-start = ((), (), s32[]{:S(2)}) async-start(), calls=%async_computation.11 | async-start | bytes 262144 | tf_op jit(solution)/shard_map/psum | solution.py:67
  1692.5 122.3 %all-gather.53.cloned.1.call-start = ((), (), s32[]{:S(2)}) async-start(), calls=%async_computation.26 | async-start | bytes 2162688 | tf_op jit(solution)/shard_map/all_gather | solution.py:72
  1766.3 125.8 %all-reduce.39.cloned.1.call-start = ((), (), s32[]{:S(2)}) async-start(), calls=%async_computation.12 | async-start | bytes 262144 | tf_op jit(solution)/shard_map/psum | solution.py:67
  1820.3 122.4 %all-gather.55.cloned.1.call-start = ((), (), s32[]{:S(2)}) async-start(), calls=%async_computation.27 | async-start | bytes 2162688 | tf_op jit(solution)/shard_map/all_gather | solution.py:72
  1894.1 126.2 %all-reduce.41.cloned.1.call-start = ((), (), s32[]{:S(2)}) async-start(), calls=%async_computation.13 | async-start | bytes 262144 | tf_op jit(solution)/shard_map/psum | solution.py:67
  1946.0 75.6 %copy-start.5 = (f32[256,128]{1,0:T(8,128)S(1)}, f32[256,128]{1,0:T(8,128)}, u32[]{:S(2)}) copy-start(f32[256,128]{1,0:T(8,128)} %get-tuple-element.39) | copy-start | bytes 393220
  1946.0 75.6 %copy-start.4 = (f32[256,128]{1,0:T(8,128)S(1)}, f32[256,128]{1,0:T(8,128)}, u32[]{:S(2)}) copy-start(f32[256,128]{1,0:T(8,128)} %get-tuple-element.37) | copy-start | bytes 393220
  1946.0 75.6 %copy-start.3 = (f32[256,128]{1,0:T(8,128)S(1)}, f32[256,128]{1,0:T(8,128)}, u32[]{:S(2)}) copy-start(f32[256,128]{1,0:T(8,128)} %get-tuple-element.35) | copy-start | bytes 393220
  1946.0 75.6 %copy-start.2 = (f32[256,128]{1,0:T(8,128)S(1)}, f32[256,128]{1,0:T(8,128)}, u32[]{:S(2)}) copy-start(f32[256,128]{1,0:T(8,128)} %get-tuple-element.33) | copy-start | bytes 393220
Sparse Core Ops, SparseCore 0:
  17.9 116.0 all-reduce.14
  136.1 39.6 all-gather.28
  179.7 112.2 all-reduce.16
  294.1 39.6 all-gather.30
  337.8 112.2 all-reduce.18
  452.2 39.6 all-gather.32
  496.0 112.2 all-reduce.20
  610.4 39.6 all-gather.34
  655.0 112.2 all-reduce.22
  769.4 39.6 all-gather.36
  813.3 112.2 all-reduce.24
  927.7 39.6 all-gather.38
  971.8 112.2 all-reduce.26
  1086.2 39.6 all-gather.40
  1128.6 48.6 all-gather.42
  1182.3 71.6 all-reduce.28
  1256.3 47.9 all-gather.44
  1309.4 71.6 all-reduce.30
  1383.9 47.9 all-gather.46
  1437.1 71.6 all-reduce.32
  1511.3 47.9 all-gather.48
  1564.6 71.6 all-reduce.34
  1639.1 47.9 all-gather.50
  1692.6 71.6 all-reduce.36
  1766.8 47.9 all-gather.52
  1820.4 71.6 all-reduce.38
  1894.7 47.9 all-gather.54
  1948.5 71.6 all-reduce.40
